TPU v7x, 32 devices: a whole 2x2x4 slice. The times are simulated.
32 devices in a mesh: tensor: 4 (over z), example: 8 (over y, x, core).
Axes of the slice: x: 2, y: 2, z: 4, core: 2. Of those that a mesh axis runs over, the one named last changes fastest.
Arguments:
- queries: bfloat16 [1, 4096, 4096], P(None, 'example', 'tensor'), may hold values from -0.0014648438 to 0.0014648438
- basis_out: bfloat16 [4096, 4096], P('example', 'tensor'), may hold values from -0.09375 to 0.09375
- basis_in: bfloat16 [4096, 4096], P('tensor', 'example'), may hold values from -0.09375 to 0.09375
- eigvals: float32 [4096, 4096], P('tensor', 'example'), may hold values from 0.25 to 4
- input_fac: bfloat16 [128, 8, 4096], P('example', None, 'tensor'), may hold values from -6 to 6
- grad_fac: bfloat16 [128, 8, 4096], P('example', None, 'tensor'), may hold values from -6 to 6
- cand_slot: int32 [128], replicated, may hold values from 0 to 127, as said below
- score_list: int32 [8, 16], replicated, may hold values from 0 to 127, as said below
- token_count: int32 [128], replicated, may hold values from 1 to 8
Outputs:
- scores: float32 [1, 128, 8], P(None, 'example')
Inputs may be any that keep to these rules, and one draw needn't show every extreme that they name: `cand_slot`: a permutation; slot s belongs to owner s // 16. `score_list`: every candidate appears exactly once; a scorer's list holds at most 4 candidates of any one owner, and some scorer takes exactly 4 from some owner.
All inputs are finite; a program needn't handle non-finite values.
Results may differ from a plain program's by a relative error of at most 0.019.
Values may be sent and summed in bfloat16 or wider, within the bound.
A program may use at most 128 MiB of HBM per device.

v0:
```python
import jax
import jax.numpy as jnp
from jax import lax
from jax.sharding import PartitionSpec as P

BF = jnp.bfloat16
F32 = jnp.float32


def regroup_grads(grads, n_tensor, n_example):
    ratio = n_example // n_tensor
    half = grads.shape[1] // ratio
    parity = lax.axis_index("example") % ratio
    received = []
    for shift in range(ratio):
        piece = lax.dynamic_slice_in_dim(grads, (parity + shift) % ratio * half, half, 1)
        perm = []
        for t in range(n_tensor):
            for e in range(n_example):
                target = e // ratio * n_example + ratio * t + (e + shift) % ratio
                perm.append((t * n_example + e, target))
        received.append(lax.ppermute(piece, ("tensor", "example"), perm))
    stacked = jnp.stack(received)
    order = (parity - jnp.arange(ratio)) % ratio
    pieces = [lax.dynamic_index_in_dim(stacked, order[p], 0, keepdims=False) for p in range(ratio)]
    return jnp.concatenate(pieces, axis=0)


def body(
    queries, basis_out, basis_in, eigvals, input_fac, grad_fac, cand_slot, score_list, token_count
):
    n_example = lax.axis_size("example")
    n_tensor = lax.axis_size("tensor")
    my_index = lax.axis_index("example")
    cand_total = cand_slot.shape[0]
    token_len = input_fac.shape[1]
    list_len = score_list.shape[1]
    query_total, rows, width = queries.shape
    acts = input_fac.reshape(-1, width)
    grads = grad_fac.reshape(-1, width)
    tokens = acts.shape[0]
    in_rows = lax.all_gather(basis_in, "example", axis=1, tiled=True)
    moved_grads = regroup_grads(grads, n_tensor, n_example)
    out_rows = lax.all_gather(basis_out, "tensor", axis=1, tiled=True)
    left = jnp.concatenate([queries.reshape(-1, width), acts], axis=0)
    half_rotated = lax.psum_scatter(
        jnp.einsum("jl,rj->lr", in_rows, left, preferred_element_type=F32).astype(BF),
        "tensor",
        scatter_dimension=0,
        tiled=True,
    )
    split = query_total * rows
    acts_rot = lax.all_gather(half_rotated[:, split:], "example", axis=0)
    parts = [half_rotated[:, q * rows : (q + 1) * rows] for q in range(query_total)]
    right = jnp.concatenate(parts + [moved_grads], axis=0)
    core = lax.psum_scatter(
        jnp.einsum("ik,xi->kx", out_rows, right, preferred_element_type=F32).astype(BF),
        "example",
        scatter_dimension=0,
        tiled=True,
    )
    wide = half_rotated.shape[0]
    grads_rot = lax.all_gather(core[:, query_total * wide :], "tensor", axis=0)
    acts_flat = jnp.transpose(acts_rot, (1, 0, 2)).reshape(wide, -1).astype(F32)
    grads_flat = jnp.transpose(grads_rot, (1, 0, 2)).reshape(core.shape[0], -1)
    partial = []
    for q in range(query_total):
        scaled = (core[:, q * wide : (q + 1) * wide].astype(F32) / eigvals.T).astype(BF)
        weighted = jnp.einsum("kl,kt->lt", scaled, grads_flat, preferred_element_type=F32)
        partial.append(jnp.sum(weighted * acts_flat, axis=0))
    summed = lax.psum(jnp.stack(partial), ("tensor", "example"))
    by_slot = summed.reshape(query_total, cand_total, token_len)
    my_list = lax.dynamic_index_in_dim(score_list, my_index, 0, keepdims=False)
    ids = jnp.arange(cand_total, dtype=jnp.int32)
    matches = my_list[:, None] == ids[None, :]
    my_slot = jnp.sum(jnp.where(matches, cand_slot[None, :], 0), axis=1)
    my_count = jnp.sum(jnp.where(matches, token_count[None, :], 0), axis=1)
    pick = my_slot[:, None] == ids[None, :]
    scores = jnp.sum(jnp.where(pick[None, :, :, None], by_slot[:, None], F32(0.0)), axis=2)
    live = jnp.arange(token_len, dtype=jnp.int32)[None, :] < my_count[:, None]
    return jnp.where(live[None], scores, F32(0.0))


def solution(mesh):
    in_specs = (
        P(None, "example", "tensor"),
        P("example", "tensor"),
        P("tensor", "example"),
        P("tensor", "example"),
        P("example", None, "tensor"),
        P("example", None, "tensor"),
        P(),
        P(),
        P(),
    )
    out_specs = P(None, "example", None)
    return jax.shard_map(body, mesh=mesh, in_specs=in_specs, out_specs=out_specs, check_vma=False)
```

profile of v0, /device:TPU:0, one launch (start us, length us, event | category | flops | bytes accessed | tf_op | source)
XLA Modules:
  0.0 471.9 jit_solution(15291793643969894554)
XLA Ops:
  6.5 0.7 all-gather.7.cloned.1.call-update
  7.3 60.6 %all-gather.7.cloned.1.call-done = bf16[1024,4096]{1,0:T(8,128)(2,1)} async-done(((bf16[1024,512]{1,0:T(8,128)(2,1)}), bf16[1024,4096]{1,0:T(8,128)(2,1)}) %all-gather.7.cloned.1.call-update) | async-done | bytes 8388624 | tf_op jit(solution)/shard_map/all_gather | solution.py:42
  67.9 9.9 %fusion.1 = bf16[4096,640]{0,1:T(8,128)(2,1)} fusion(bf16[1024,4096]{1,0:T(8,128)(2,1)} %all-gather.7.cloned.1.call-done, bf16[128,1024]{1,0:T(8,128)(2,1)} %bitcast.54, bf16[512,1024]{1,0:T(8,128)(2,1)} %bitcast.53), kind=kOutput, calls=%fused_computation.3 | convolution fusion | flops 5373952000 | bytes 14942208 | tf_op jit(solution)/shard_map/jl,rj->lr/dot_general | solution.py:47
  77.9 0.7 all-gather.9.cloned.1.call-update
  78.7 0.1 copy-done.1
  78.8 0.1 copy.23
  78.9 0.7 collective-permute-start
  79.6 0.1 copy.24
  79.7 0.3 collective-permute-start.1
  80.0 0.6 fusion.22
  84.5 0.1 fusion.17
  84.6 102.3 %reduce-scatter.3.cloned.1.call-done = bf16[1024,640]{0,1:T(8,128)(2,1)} async-done(((bf16[4096,640]{0,1:T(8,128)(2,1)}), bf16[1024,640]{0,1:T(8,128)(2,1)}) %reduce-scatter.3.cloned.1.call-update) | async-done | bytes 1310736 | tf_op jit(solution)/shard_map/reduce_scatter | solution.py:46
  186.9 1.3 slice.24
  188.2 80.4 %all-gather.9.cloned.1.call-done = bf16[512,4096]{1,0:T(8,128)(2,1)} async-done(((bf16[512,1024]{1,0:T(8,128)(2,1)}), bf16[512,4096]{1,0:T(8,128)(2,1)}) %all-gather.9.cloned.1.call-update) | async-done | bytes 4194320 | tf_op jit(solution)/shard_map/all_gather | solution.py:44
  268.6 10.5 %fusion = bf16[4096,1280]{0,1:T(8,128)(2,1)} fusion(bf16[512,4096]{1,0:T(8,128)(2,1)} %all-gather.9.cloned.1.call-done, bf16[128,512]{0,1:T(8,128)(2,1)S(1)} %get-tuple-element.8, bf16[128,512]{0,1:T(8,128)(2,1)S(1)} %get-tuple-element.7, bf16[1024,512]{0,1:T(8,128)(2,1)S(1)} %slice.24), kind=kOutput, calls=%fused_computation.1 | convolution fusion | flops 5377884160 | bytes 15990784 | tf_op jit(solution)/shard_map/ik,xi->kx/dot_general | solution.py:57
  279.2 1.7 slice.27
  280.9 0.2 all-gather.11.cloned.1.call-start
  281.2 78.3 %reduce-scatter.5.cloned.1.call-done = bf16[512,1280]{0,1:T(8,128)(2,1)} async-done(((bf16[4096,1280]{0,1:T(8,128)(2,1)}), bf16[512,1280]{0,1:T(8,128)(2,1)}) %reduce-scatter.5.cloned.1.call-update) | async-done | bytes 1310736 | tf_op jit(solution)/shard_map/reduce_scatter | solution.py:56
  359.4 1.7 slice.26
  361.1 0.2 select_reduce_fusion.2
  361.3 0.1 iota_compare_fusion
  361.4 27.7 %all-gather.13.cloned.1.call-done = bf16[8192,128]{0,1:T(8,128)(2,1)} async-done(((bf16[1024,128]{0,1:T(8,128)(2,1)}), bf16[8192,128]{0,1:T(8,128)(2,1)}) %all-gather.13.cloned.1.call-update) | async-done | bytes 2097168 | tf_op jit(solution)/shard_map/all_gather | solution.py:53
  389.1 2.0 convert_element_type.38
  391.1 5.3 %copy.26 = f32[16,8,8,1024]{3,2,1,0:T(8,128)} copy(f32[16,8,8,1024]{3,1,2,0:T(8,128)S(1)} %bitcast.45) | data formatting | bytes 8388608
  396.4 5.9 %copy.20 = f32[1024,8,128]{2,1,0:T(8,128)} copy(f32[1024,8,128]{0,1,2:T(8,128)} %bitcast.46) | data formatting | bytes 8388608 | tf_op jit(solution)/shard_map/convert_element_type | solution.py:64
  402.4 16.1 %all-gather.11.cloned.1.call-done = bf16[2048,256]{0,1:T(8,128)(2,1)} async-done(((bf16[512,256]{0,1:T(8,128)(2,1)}), bf16[2048,256]{0,1:T(8,128)(2,1)}) %all-gather.11.cloned.1.call-update) | async-done | bytes 1048592 | tf_op jit(solution)/shard_map/all_gather | solution.py:63
  418.5 1.3 copy.30
  419.8 3.9 fusion.2
  423.7 0.1 broadcast_in_dim.58
  423.8 40.5 %psum.7 = f32[128,8]{1,0:T(8,128)S(1)} all-reduce(f32[128,8]{1,0:T(8,128)S(1)} %broadcast_in_dim.58), channel_id=1, replica_groups=mesh['tensor'=4,'example'=8] {'tensor','example'}, use_global_device_ids=true, to_apply=%region_5.6 | all-reduce | flops 1024 | bytes 8192 | tf_op jit(solution)/shard_map/psum | solution.py:71
  464.3 0.1 select_reduce_fusion
  464.5 0.6 bitcast_select_fusion
  (27 shorter events, 0.4 us)
Async XLA Ops:
  6.5 354.6 %copy-start = (s32[8,16]{1,0:T(8,128)S(1)}, s32[8,16]{1,0:T(8,128)}, u32[]{:S(2)}) copy-start(s32[8,16]{1,0:T(8,128)} %param.16) | copy-start | bytes 1540
  6.5 61.4 %all-gather.7.cloned.1.call-start = ((), (), s32[]{:S(2)}) async-start(), calls=%async_computation.2 | async-start | bytes 9437184 | tf_op jit(solution)/shard_map/all_gather | solution.py:42
  7.3 179.7 %reduce-scatter.3.cloned.1.call-start = ((), (), s32[]{:S(2)}) async-start(), calls=%async_computation.3 | async-start | bytes 6553600 | tf_op jit(solution)/shard_map/reduce_scatter | solution.py:46
  77.8 0.9 copy-start.1
  77.8 190.8 %all-gather.9.cloned.1.call-start = ((), (), s32[]{:S(2)}) async-start(), calls=%async_computation.4 | async-start | bytes 5242880 | tf_op jit(solution)/shard_map/all_gather | solution.py:44
  78.6 280.9 %reduce-scatter.5.cloned.1.call-start = ((), (), s32[]{:S(2)}) async-start(), calls=%async_computation.5 | async-start | bytes 11796480 | tf_op jit(solution)/shard_map/reduce_scatter | solution.py:56
  78.9 5.6 %collective-permute-start = (bf16[128,512]{0,1:T(8,128)(2,1)S(1)}, bf16[128,512]{0,1:T(8,128)(2,1)S(1)}, u32[]{:S(2)}, u32[]{:S(2)}) collective-permute-start(bf16[128,512]{0,1:T(8,128)(2,1)S(1)} %copy.23), channel_id=1, source_target_pairs={{0,0},{1,1},{2,8},{3,9},{4,16},{5,17},{6,24},{7,25},{8,2},{9,3},{1... | collective-permute-start | bytes 393224 | tf_op jit(solution)/shard_map/ppermute | solution.py:22
  79.7 4.8 %collective-permute-start.1 = (bf16[128,512]{0,1:T(8,128)(2,1)S(1)}, bf16[128,512]{0,1:T(8,128)(2,1)S(1)}, u32[]{:S(2)}, u32[]{:S(2)}) collective-permute-start(bf16[128,512]{0,1:T(8,128)(2,1)S(1)} %copy.24), channel_id=1, source_target_pairs={{0,1},{1,0},{2,9},{3,8},{4,17},{5,16},{6,25},{7,24},{8,3},{9,2},{1... | collective-permute-start | bytes 393224 | tf_op jit(solution)/shard_map/ppermute | solution.py:22
  279.1 82.0 %copy-start.3 = (s32[128]{0:T(128)S(1)}, s32[128]{0:T(128)}, u32[]{:S(2)}) copy-start(s32[128]{0:T(128)} %param.17) | copy-start | bytes 1540
  279.1 82.0 %copy-start.4 = (s32[128]{0:T(128)S(1)}, s32[128]{0:T(128)}, u32[]{:S(2)}) copy-start(s32[128]{0:T(128)} %param.15) | copy-start | bytes 1540
  279.2 109.9 %all-gather.13.cloned.1.call-start = ((), (), s32[]{:S(2)}) async-start(), calls=%async_computation.7 | async-start | bytes 2359296 | tf_op jit(solution)/shard_map/all_gather | solution.py:53
  280.9 137.5 %all-gather.11.cloned.1.call-start = ((), (), s32[]{:S(2)}) async-start(), calls=%async_computation.6 | async-start | bytes 1310720 | tf_op jit(solution)/shard_map/all_gather | solution.py:63
  396.4 23.4 %copy-start.2 = (bf16[512,1280]{0,1:T(8,128)(2,1)S(1)}, bf16[512,1280]{0,1:T(8,128)(2,1)}, u32[]{:S(2)}) copy-start(bf16[512,1280]{0,1:T(8,128)(2,1)} %reduce-scatter.5.cloned.1.call-done) | copy-start | bytes 3932164
  396.4 23.4 %copy-start.5 = (f32[1024,512]{1,0:T(8,128)S(1)}, f32[1024,512]{1,0:T(8,128)}, u32[]{:S(2)}) copy-start(f32[1024,512]{1,0:T(8,128)} %param.12) | copy-start | bytes 6291460
Sparse Core Ops, SparseCore 0:
  9.2 58.6 all-gather.6
  77.9 108.9 reduce-scatter.2
  188.5 80.0 all-gather.8
  279.3 80.0 reduce-scatter.4
  361.2 27.8 all-gather.12
  390.5 27.9 all-gather.10
where the time goes:
time: 472 us
  waiting for transfers between devices  367 us (78%)
  blocking collectives  40.5 us (9%)
  matrix products  24.3 us (5%)
  local copies, waits for them, and re-layouts  18.4 us (4%)
  between operations  17.5 us (4%)
    reduce_scatter x1, waiting for transfers between devices, body(): lax.psum_scatter(jnp.einsum('jl,rj->lr', in_rows, left, preferred_element...  102 us
    all_gather x1, waiting for transfers between devices, body(): out_rows = lax.all_gather(basis_out, 'tensor', axis=1, tiled=True)  80.4 us
    reduce_scatter x1, waiting for transfers between devices, body(): lax.psum_scatter(jnp.einsum('ik,xi->kx', out_rows, right, preferred_eleme...  78.3 us
    all_gather x1, waiting for transfers between devices, body(): in_rows = lax.all_gather(basis_in, 'example', axis=1, tiled=True)  60.6 us
    psum x1, blocking collectives, body(): summed = lax.psum(jnp.stack(partial), ('tensor', 'example'))  40.5 us
    all_gather x1, waiting for transfers between devices, body(): acts_rot = lax.all_gather(half_rotated[:, split:], 'example', axis=0)  27.7 us
    all_gather x1, waiting for transfers between devices, body(): grads_rot = lax.all_gather(core[:, query_total * wide:], 'tensor', axis=0)  16.1 us
    dot_general x1, matrix products, body(): jnp.einsum('ik,xi->kx', out_rows, right, preferred_element_type=F32)  10.5 us
  transfers between devices with their start and end apart: 8, of which 6 were waited for; matrix products, arithmetic and copies ran while one was open for 4% of the time, Pallas kernels for 0%

commit v1 on v0

--- a/solution.py
+++ b/solution.py
@@ -1,3 +1,4 @@
+import functools
 import jax
 import jax.numpy as jnp
 from jax import lax
@@ -5,6 +6,26 @@
 
 BF = jnp.bfloat16
 F32 = jnp.float32
+
+
+def measure_the_object(array_here, chip_axis, dim_i):
+    vals = []
+    sides = lax.axis_size(chip_axis)
+    for dd in range(sides):
+        vals.append((dd, (dd + 1) % sides))
+
+    def map_outputs_here(z):
+        if len(z) == sides:
+            return z
+        w1 = map_outputs_here([lax.ppermute(z[0], chip_axis, perm=vals), *z])
+        return w1
+
+    val2 = jnp.concatenate(map_outputs_here([array_here]), dim_i)
+    later = jnp.roll(val2, (lax.axis_index(chip_axis) + 1) * array_here.shape[dim_i], dim_i)
+    return later
+
+
+refer_sums_all_by_axis = functools.partial(measure_the_object, chip_axis="tensor", dim_i=1)
 
 
 def regroup_grads(grads, n_tensor, n_example):
@@ -41,7 +62,7 @@
     tokens = acts.shape[0]
     in_rows = lax.all_gather(basis_in, "example", axis=1, tiled=True)
     moved_grads = regroup_grads(grads, n_tensor, n_example)
-    out_rows = lax.all_gather(basis_out, "tensor", axis=1, tiled=True)
+    out_rows = refer_sums_all_by_axis(basis_out)
     left = jnp.concatenate([queries.reshape(-1, width), acts], axis=0)
     half_rotated = lax.psum_scatter(
         jnp.einsum("jl,rj->lr", in_rows, left, preferred_element_type=F32).astype(BF),

time: 472 us -> 470 us (level)
  waiting for transfers between devices: 367 us -> 311 us
  starting transfers between devices: 1.38 us -> 37.9 us
  local copies, waits for them, and re-layouts: 18.4 us -> 33.3 us
    ppermute x0 -> x3, waiting for transfers between devices: none -> 113 us  [map_outputs_here(): w1 = map_outputs_here([lax.ppermute(z[0], chip_axis, perm=vals), *z])]
    reduce_scatter x1, waiting for transfers between devices: 102 us -> 0.87 us  [body(): lax.psum_scatter(jnp.einsum('jl,rj->lr', in_rows, left, preferred_element...]
    all_gather x1 -> x0, waiting for transfers between devices: 80.4 us -> none  [body(): out_rows = lax.all_gather(basis_out, 'tensor', axis=1, tiled=True)]
    ppermute x0 -> x3, starting transfers between devices: none -> 36.1 us  [map_outputs_here(): w1 = map_outputs_here([lax.ppermute(z[0], chip_axis, perm=vals), *z])]
    reduce_scatter x1, waiting for transfers between devices: 78.3 us -> 93.2 us  [body(): lax.psum_scatter(jnp.einsum('ik,xi->kx', out_rows, right, preferred_eleme...]
    unnamed x15 -> x23, local copies, waits for them, and re-layouts: 5.69 us -> 18.5 us
  transfers between devices with their start and end apart: 8 -> 10, of which waited for: 6 -> 8; matrix products, arithmetic and copies ran while one was open for 4% -> 7% of each run, Pallas kernels for 0% -> 0%
where the time goes in v1:
time: 470 us; the launch traced here: 469 us
  waiting for transfers between devices  311 us (66%)
  blocking collectives  40.5 us (9%)
  starting transfers between devices  37.9 us (8%)
  local copies, waits for them, and re-layouts  33.3 us (7%)
  matrix products  25.7 us (5%)
  between operations  17.3 us (4%)
    ppermute x3, waiting for transfers between devices, map_outputs_here(): w1 = map_outputs_here([lax.ppermute(z[0], chip_axis, perm=vals), *z])  113 us
    reduce_scatter x1, waiting for transfers between devices, body(): lax.psum_scatter(jnp.einsum('ik,xi->kx', out_rows, right, preferred_eleme...  93.2 us
    all_gather x1, waiting for transfers between devices, body(): in_rows = lax.all_gather(basis_in, 'example', axis=1, tiled=True)  60.6 us
    psum x1, blocking collectives, body(): summed = lax.psum(jnp.stack(partial), ('tensor', 'example'))  40.5 us
    ppermute x3, starting transfers between devices, map_outputs_here(): w1 = map_outputs_here([lax.ppermute(z[0], chip_axis, perm=vals), *z])  36.1 us
    all_gather x1, waiting for transfers between devices, body(): acts_rot = lax.all_gather(half_rotated[:, split:], 'example', axis=0)  25.8 us
    unnamed x23, local copies, waits for them, and re-layouts  18.5 us
    all_gather x1, waiting for transfers between devices, body(): grads_rot = lax.all_gather(core[:, query_total * wide:], 'tensor', axis=0)  16.5 us
  transfers between devices with their start and end apart: 10, of which 8 were waited for; matrix products, arithmetic and copies ran while one was open for 7% of the time, Pallas kernels for 0%

profile of v1, /device:TPU:0, one launch (start us, length us, event | category | flops | bytes accessed | tf_op | source)
XLA Modules:
  0.0 469.4 jit_solution(11210910966735715808)
XLA Ops:
  7.3 60.6 %all-gather.6.cloned.1.call-done = bf16[1024,4096]{1,0:T(8,128)(2,1)} async-done(((bf16[1024,512]{1,0:T(8,128)(2,1)}), bf16[1024,4096]{1,0:T(8,128)(2,1)}) %all-gather.6.cloned.1.call-update) | async-done | bytes 8388624 | tf_op jit(solution)/shard_map/all_gather | solution.py:63
  67.9 9.8 %fusion = bf16[4096,640]{0,1:T(8,128)(2,1)} fusion(bf16[1024,4096]{1,0:T(8,128)(2,1)} %all-gather.6.cloned.1.call-done, bf16[128,1024]{1,0:T(8,128)(2,1)} %bitcast.47, bf16[512,1024]{1,0:T(8,128)(2,1)} %bitcast.46), kind=kOutput, calls=%fused_computation.2 | convolution fusion | flops 5373952000 | bytes 14942208 | tf_op jit(solution)/shard_map/jl,rj->lr/dot_general | solution.py:68
  77.8 1.1 copy-done.1
  79.0 1.5 collective-permute-start
  80.5 44.6 %collective-permute-done = bf16[512,1024]{1,0:T(8,128)(2,1)S(1)} collective-permute-done((bf16[512,1024]{1,0:T(8,128)(2,1)S(1)}, bf16[512,1024]{1,0:T(8,128)(2,1)S(1)}, u32[]{:S(2)}, u32[]{:S(2)}) %collective-permute-start) | collective-permute-done | bytes 1048608 | tf_op jit(solution)/shard_map/ppermute | solution.py:20
  125.0 17.2 %collective-permute-start.1 = (bf16[512,1024]{1,0:T(8,128)(2,1)S(1)}, bf16[512,1024]{1,0:T(8,128)(2,1)S(1)}, u32[]{:S(2)}, u32[]{:S(2)}) collective-permute-start(bf16[512,1024]{1,0:T(8,128)(2,1)S(1)} %collective-permute-done), channel_id=1, source_target_pairs={{0,8},{8,16},{16,24},{24,0},{1,9},{9,17},{17,25},{25,1},{2,10},{10... | collective-permute-start | bytes 3145736 | tf_op jit(solution)/shard_map/ppermute | solution.py:20
  142.2 48.4 %collective-permute-done.1 = bf16[512,1024]{1,0:T(8,128)(2,1)S(1)} collective-permute-done((bf16[512,1024]{1,0:T(8,128)(2,1)S(1)}, bf16[512,1024]{1,0:T(8,128)(2,1)S(1)}, u32[]{:S(2)}, u32[]{:S(2)}) %collective-permute-start.1) | collective-permute-done | bytes 1048608 | tf_op jit(solution)/shard_map/ppermute | solution.py:20
  190.6 17.4 %collective-permute-start.2 = (bf16[512,1024]{1,0:T(8,128)(2,1)S(1)}, bf16[512,1024]{1,0:T(8,128)(2,1)}, u32[]{:S(2)}, u32[]{:S(2)}) collective-permute-start(bf16[512,1024]{1,0:T(8,128)(2,1)S(1)} %collective-permute-done.1), channel_id=1, source_target_pairs={{0,8},{8,16},{16,24},{24,0},{1,9},{9,17},{17,25},{25,1},{2,10},{10... | collective-permute-start | bytes 3145736 | tf_op jit(solution)/shard_map/ppermute | solution.py:20
  209.1 1.3 collective-permute-start.3
  216.4 20.0 %collective-permute-done.2 = bf16[512,1024]{1,0:T(8,128)(2,1)} collective-permute-done((bf16[512,1024]{1,0:T(8,128)(2,1)S(1)}, bf16[512,1024]{1,0:T(8,128)(2,1)}, u32[]{:S(2)}, u32[]{:S(2)}) %collective-permute-start.2) | collective-permute-done | bytes 1048608 | tf_op jit(solution)/shard_map/ppermute | solution.py:20
  236.3 2.3 constant_dynamic-update-slice_fusion.7
  238.7 1.1 constant_dynamic-update-slice_fusion.6
  239.8 1.1 constant_dynamic-update-slice_fusion.5
  240.8 1.1 constant_dynamic-update-slice_fusion.4
  241.9 2.3 constant_dynamic-update-slice_fusion.3
  244.2 1.1 constant_dynamic-update-slice_fusion.2
  245.3 1.1 constant_dynamic-update-slice_fusion.1
  246.4 1.1 constant_dynamic-update-slice_fusion
  248.3 1.3 slice.24
  249.6 11.7 %convolution_convert_fusion = bf16[4096,1280]{1,0:T(8,128)(2,1)} fusion(bf16[512,8192]{1,0:T(8,128)(2,1)} %constant_dynamic-update-slice_fusion, s32[]{:T(128)S(6)} %select_n.85, bf16[128,512]{0,1:T(8,128)(2,1)S(1)} %get-tuple-element.8, bf16[128,512]{0,1:T(8,128)(2,1)S(1)} %get-tuple-element.7, bf16[1024,512]{0,1:T(8,128)(2,1)S(1)} %slice.24), kind=kOutput, calls=%fused_computation | convolution fusion | flops 5377884160 | bytes 15990788 | tf_op jit(solution)/shard_map/ik,xi->kx/dot_general | solution.py:78
  261.5 1.8 slice.27
  263.5 93.2 %reduce-scatter.5.cloned.1.call-done = bf16[512,1280]{1,0:T(8,128)(2,1)} async-done(((bf16[4096,1280]{1,0:T(8,128)(2,1)}), bf16[512,1280]{1,0:T(8,128)(2,1)}) %reduce-scatter.5.cloned.1.call-update) | async-done | bytes 1310736 | tf_op jit(solution)/shard_map/reduce_scatter | solution.py:77
  356.8 1.7 slice.26
  358.5 1.9 copy.21
  360.6 25.8 %all-gather.10.cloned.1.call-done = bf16[8192,128]{0,1:T(8,128)(2,1)} async-done(((bf16[1024,128]{0,1:T(8,128)(2,1)}), bf16[8192,128]{0,1:T(8,128)(2,1)}) %all-gather.10.cloned.1.call-update) | async-done | bytes 2097168 | tf_op jit(solution)/shard_map/all_gather | solution.py:74
  386.4 2.0 convert_element_type.34
  388.4 5.2 %copy.28 = f32[16,8,8,1024]{3,2,1,0:T(8,128)} copy(f32[16,8,8,1024]{3,1,2,0:T(8,128)S(1)} %bitcast.39) | data formatting | bytes 8388608
  393.7 5.6 %copy.23 = f32[1024,8,128]{2,1,0:T(8,128)} copy(f32[1024,8,128]{0,1,2:T(8,128)} %bitcast.40) | data formatting | bytes 8388608 | tf_op jit(solution)/shard_map/convert_element_type | solution.py:85
  399.3 16.5 %all-gather.8.cloned.1.call-done = bf16[2048,256]{1,0:T(8,128)(2,1)} async-done(((bf16[512,256]{1,0:T(8,128)(2,1)}), bf16[2048,256]{1,0:T(8,128)(2,1)}) %all-gather.8.cloned.1.call-update) | async-done | bytes 1048592 | tf_op jit(solution)/shard_map/all_gather | solution.py:84
  415.8 1.5 copy.22
  417.3 4.2 fusion.1
  421.6 40.5 %psum.7 = f32[128,8]{1,0:T(8,128)S(1)} all-reduce(f32[128,8]{1,0:T(8,128)S(1)} %broadcast_in_dim.58), channel_id=1, replica_groups=mesh['tensor'=4,'example'=8] {'tensor','example'}, use_global_device_ids=true, to_apply=%region_5.6 | all-reduce | flops 1024 | bytes 8192 | tf_op jit(solution)/shard_map/psum | solution.py:92
  (39 shorter events, 6.2 us)
Async XLA Ops:
  6.5 353.8 %copy-start = (s32[8,16]{1,0:T(8,128)S(1)}, s32[8,16]{1,0:T(8,128)}, u32[]{:S(2)}) copy-start(s32[8,16]{1,0:T(8,128)} %param.16) | copy-start | bytes 1540
  6.5 61.4 %all-gather.6.cloned.1.call-start = ((), (), s32[]{:S(2)}) async-start(), calls=%async_computation.2 | async-start | bytes 9437184 | tf_op jit(solution)/shard_map/all_gather | solution.py:63
  7.3 241.1 %reduce-scatter.3.cloned.1.call-start = ((), (), s32[]{:S(2)}) async-start(), calls=%async_computation.3 | async-start | bytes 6553600 | tf_op jit(solution)/shard_map/reduce_scatter | solution.py:67
  77.8 1.2 copy-start.1
  77.8 279.0 %reduce-scatter.5.cloned.1.call-start = ((), (), s32[]{:S(2)}) async-start(), calls=%async_computation.4 | async-start | bytes 11796480 | tf_op jit(solution)/shard_map/reduce_scatter | solution.py:77
  79.0 46.0 %collective-permute-start = (bf16[512,1024]{1,0:T(8,128)(2,1)S(1)}, bf16[512,1024]{1,0:T(8,128)(2,1)S(1)}, u32[]{:S(2)}, u32[]{:S(2)}) collective-permute-start(bf16[512,1024]{1,0:T(8,128)(2,1)S(1)} %copy-done.1), channel_id=1, source_target_pairs={{0,8},{8,16},{16,24},{24,0},{1,9},{9,17},{17,25},{25,1},{2,10},{10... | collective-permute-start | bytes 3145736 | tf_op jit(solution)/shard_map/ppermute | solution.py:20
  125.0 65.6 %collective-permute-start.1 = (bf16[512,1024]{1,0:T(8,128)(2,1)S(1)}, bf16[512,1024]{1,0:T(8,128)(2,1)S(1)}, u32[]{:S(2)}, u32[]{:S(2)}) collective-permute-start(bf16[512,1024]{1,0:T(8,128)(2,1)S(1)} %collective-permute-done), channel_id=1, source_target_pairs={{0,8},{8,16},{16,24},{24,0},{1,9},{9,17},{17,25},{25,1},{2,10},{10... | collective-permute-start | bytes 3145736 | tf_op jit(solution)/shard_map/ppermute | solution.py:20
  190.6 45.7 %collective-permute-start.2 = (bf16[512,1024]{1,0:T(8,128)(2,1)S(1)}, bf16[512,1024]{1,0:T(8,128)(2,1)}, u32[]{:S(2)}, u32[]{:S(2)}) collective-permute-start(bf16[512,1024]{1,0:T(8,128)(2,1)S(1)} %collective-permute-done.1), channel_id=1, source_target_pairs={{0,8},{8,16},{16,24},{24,0},{1,9},{9,17},{17,25},{25,1},{2,10},{10... | collective-permute-start | bytes 3145736 | tf_op jit(solution)/shard_map/ppermute | solution.py:20
  209.1 6.2 %collective-permute-start.3 = (bf16[128,512]{0,1:T(8,128)(2,1)S(1)}, bf16[128,512]{0,1:T(8,128)(2,1)}, u32[]{:S(2)}, u32[]{:S(2)}) collective-permute-start(bf16[128,512]{0,1:T(8,128)(2,1)S(1)} %copy.26), channel_id=1, source_target_pairs={{0,0},{1,1},{2,8},{3,9},{4,16},{5,17},{6,24},{7,25},{8,2},{9,3},{1... | collective-permute-start | bytes 393224 | tf_op jit(solution)/shard_map/ppermute | solution.py:43
  210.6 4.7 %collective-permute-start.4 = (bf16[128,512]{0,1:T(8,128)(2,1)S(1)}, bf16[128,512]{0,1:T(8,128)(2,1)S(1)}, u32[]{:S(2)}, u32[]{:S(2)}) collective-permute-start(bf16[128,512]{0,1:T(8,128)(2,1)S(1)} %copy.27), channel_id=1, source_target_pairs={{0,1},{1,0},{2,9},{3,8},{4,17},{5,16},{6,25},{7,24},{8,3},{9,2},{1... | collective-permute-start | bytes 393224 | tf_op jit(solution)/shard_map/ppermute | solution.py:43
  261.4 97.1 %copy-start.2 = (f32[1024,512]{1,0:T(8,128)S(1)}, f32[1024,512]{1,0:T(8,128)}, u32[]{:S(2)}) copy-start(f32[1024,512]{1,0:T(8,128)} %param.12) | copy-start | bytes 6291460
  261.4 98.9 %copy-start.4 = (s32[128]{0:T(128)S(1)}, s32[128]{0:T(128)}, u32[]{:S(2)}) copy-start(s32[128]{0:T(128)} %param.17) | copy-start | bytes 1540
  261.4 98.9 %copy-start.5 = (s32[128]{0:T(128)S(1)}, s32[128]{0:T(128)}, u32[]{:S(2)}) copy-start(s32[128]{0:T(128)} %param.15) | copy-start | bytes 1540
  261.4 125.0 %all-gather.10.cloned.1.call-start = ((), (), s32[]{:S(2)}) async-start(), calls=%async_computation.6 | async-start | bytes 2359296 | tf_op jit(solution)/shard_map/all_gather | solution.py:74
  263.3 152.5 %all-gather.8.cloned.1.call-start = ((), (), s32[]{:S(2)}) async-start(), calls=%async_computation.5 | async-start | bytes 1310720 | tf_op jit(solution)/shard_map/all_gather | solution.py:84
  393.7 23.6 %copy-start.3 = (f32[1024,512]{0,1:T(8,128)S(1)}, f32[1024,512]{0,1:T(8,128)}, u32[]{:S(2)}) copy-start(f32[1024,512]{0,1:T(8,128)} %copy.21) | copy-start | bytes 6291460
Sparse Core Ops, SparseCore 0:
  9.2 58.6 all-gather.5
  77.9 170.3 reduce-scatter.2
  261.5 95.1 reduce-scatter.4
  358.5 27.8 all-gather.9
  387.8 27.9 all-gather.7
